TPU v7x, 32 devices: a whole 2x2x4 slice. The times are simulated.
32 devices in a mesh: groups: 2 (over y), tok: 4 (over z), lay: 2 (over x), head: 2 (over core).
Axes of the slice: x: 2, y: 2, z: 4, core: 2. Of those that a mesh axis runs over, the one named last changes fastest.
Arguments:
- keys: float32 [2, 4096, 1024], P('lay', ('groups', 'tok'), 'head'), parts along dimension 1, may hold values from -80 to 80, as said below
- values: float32 [2, 4096, 1024], P('lay', ('groups', 'tok'), 'head'), parts along dimension 1, may hold values from -24 to 24
- queries: float32 [2, 32, 8192], P('lay', 'groups', 'head'), parts along dimension 1, may hold values from -620 to 620, as said below
- start_block: float32 [4096, 256], P(('groups', 'tok')), parts along dimension 0, may hold values from -6 to 6
- lengths: int32 [32], P('groups'), parts along dimension 0, may hold values from 1 to 2048, as said below
Outputs:
- attended: float32 [2, 32, 2, 4096], P('lay', 'groups', 'head', 'tok'), parts along dimension 1
There are 2 independent parts, one for each index of `groups`. A program takes and returns all parts, laid end to end along the dimension named above; each array names one. Nothing has to cross between parts.
Inputs may be any that keep to these rules, and one draw needn't show every extreme that they name: keys lie within this range. queries lie within this range. `lengths`: the longest row covers all 2048 tokens.
All inputs are finite; a program needn't handle non-finite values.
Results may differ from a plain program's by a relative error of at most 0.0003.
Values sent between devices are 32-bit elements; how exact they have to be, the bound alone decides.
No kernel may reach another device: no remote copies, remote signals or barrier semaphores. Data moves between devices by JAX's collectives and lax.ppermute only.
A program may use at most 64 MiB of HBM per device.

v0:
```python
import math
import jax
import jax.numpy as jnp
from jax import lax
from jax.sharding import PartitionSpec as P

KVH = 8
HD = 128
QH = 64
ITERS = 2
NEG = -1e30


def joined(part, axis, combine):
    gathered = jax.tree.map(lambda a: lax.all_gather(a, axis), part)

    def take(source):
        return jax.tree.map(lambda a: lax.dynamic_index_in_dim(a, source, 0, False), gathered)

    return lax.fori_loop(
        1, lax.axis_size(axis), lambda source, state: combine(state, take(source)), take(0)
    )


def gram_of(block):
    return jnp.dot(
        block.T, block, precision=lax.Precision.HIGHEST, preferred_element_type=jnp.float32
    )


def right_solve(lower, matrix):
    return lax.linalg.triangular_solve(lower, matrix, left_side=False, lower=True, transpose_a=True)


def project(keys, basis):
    return jnp.einsum("lsc,sr->lcr", keys, basis, precision=lax.Precision.HIGHEST)


def mix_block(keys, coef):
    partial_block = jnp.einsum("lsc,lcr->sr", keys, coef, precision=lax.Precision.HIGHEST)
    return lax.psum(partial_block, ("lay", "head"))


def combine(first, second):
    top = jnp.maximum(first[0], second[0])
    scale_one = jnp.exp(first[0] - top)
    scale_two = jnp.exp(second[0] - top)
    total = first[1] * scale_one + second[1] * scale_two
    summed = first[2] * scale_one[..., None] + second[2] * scale_two[..., None]
    return (top, total, summed)


def body(keys, values, queries, start_block, lengths):
    highest = lax.Precision.HIGHEST
    lay_dev, tok_dev, kv_dev = keys.shape
    rank = start_block.shape[1]
    rows = queries.shape[1]
    local_heads = queries.shape[2] // HD
    group = QH // KVH
    kv_local = kv_dev // HD

    def finish(block):
        gram, proj = lax.psum((gram_of(block), project(keys, block)), "tok")
        lower = jnp.linalg.cholesky(gram)
        coef_new = right_solve(lower, proj.reshape(-1, rank)).reshape(proj.shape)
        return (right_solve(lower, block), coef_new)

    basis, coef = finish(start_block)
    for step in range(ITERS):
        basis, coef = finish(mix_block(keys, coef))
    quer = queries.reshape(lay_dev, rows, kv_local, group, HD)
    factor = coef.reshape(lay_dev, kv_local, HD, rank)
    reduced = jnp.einsum("lbgid,lgdr->lgibr", quer, factor, precision=highest) / math.sqrt(HD)
    reduced = reduced.reshape(lay_dev, kv_local, group * rows, rank)
    scores = jnp.einsum("tr,lgxr->tlgx", basis, reduced, precision=highest)
    position = lax.axis_index("tok") * tok_dev + jnp.arange(tok_dev, dtype=jnp.int32)
    valid = position[:, None] < lengths[None, :]
    valid = jnp.tile(valid, (1, group))[:, None, None, :]
    peak = jnp.max(jnp.where(valid, scores, NEG), axis=0)
    weight = jnp.where(valid, jnp.exp(scores - peak[None]), 0.0)
    total = jnp.sum(weight, axis=0)
    vals = values.reshape(lay_dev, tok_dev, kv_local, HD)
    summed = jnp.einsum("tlgx,ltgd->lgxd", weight, vals, precision=highest)
    peak = peak.reshape(lay_dev, local_heads, rows)
    total = total.reshape(lay_dev, local_heads, rows)
    summed = summed.reshape(lay_dev, local_heads, rows, HD)
    share = local_heads // lax.axis_size("tok")
    top, whole_total, whole_sum = joined((peak, total, summed), "tok", combine)
    result = whole_sum / whole_total[..., None]
    result = lax.dynamic_slice_in_dim(result, lax.axis_index("tok") * share, share, 1)
    result = result.transpose(0, 2, 1, 3)
    return result.reshape(lay_dev, rows, 1, share * HD)


def solution(mesh):
    return jax.shard_map(
        body,
        mesh=mesh,
        in_specs=(
            P("lay", ("groups", "tok"), "head"),
            P("lay", ("groups", "tok"), "head"),
            P("lay", "groups", "head"),
            P(("groups", "tok"), None),
            P("groups"),
        ),
        out_specs=P("lay", "groups", "head", "tok"),
        check_vma=False,
    )
```

profile of v0, /device:TPU:0, one launch (start us, length us, event | category | flops | bytes accessed | tf_op | source)
XLA Modules:
  0.0 476.8 jit_solution(16566091933869575326)
XLA Ops:
  6.5 3.0 fusion.71
  9.6 2.6 fusion.9
  12.4 46.5 %all-reduce.18.cloned.1.call-done = (f32[512,256]{1,0:T(8,128)}, f32[256,256]{0,1:T(8,128)}) async-done(((f32[512,256]{1,0:T(8,128)}, f32[256,256]{0,1:T(8,128)}), (f32[512,256]{1,0:T(8,128)}, f32[256,256]{0,1:T(8,128)})) %all-reduce.18.cloned.1.call-update) | async-done | bytes 786448 | tf_op jit(solution)/shard_map/psum | solution.py:63
  59.0 1.1 copy.45
  60.2 11.7 %cholesky.172 = f32[128,128]{1,0:T(8,128)S(1)} custom-call(f32[128,128]{1,0:T(8,128)S(1)} %cholesky.270), custom_call_target="Cholesky" | custom-call | tf_op jit(solution)/shard_map/jit(cholesky)/cholesky | solution.py:64
  71.9 9.8 %custom-call.16 = f32[1,128,128]{1,2,0:T(8,128)S(1)} custom-call(f32[1,128,128]{2,1,0:T(8,128)S(1)} %get-tuple-element.288), custom_call_target="InvertDiagBlocksLowerTriangular" | custom-call | tf_op jit(solution)/shard_map/jit(cholesky)/cholesky | solution.py:64
  82.3 11.7 %cholesky.189 = f32[128,128]{1,0:T(8,128)S(1)} custom-call(f32[128,128]{1,0:T(8,128)S(1)} %convolution_subtract_fusion.6), custom_call_target="Cholesky" | custom-call | tf_op jit(solution)/shard_map/jit(cholesky)/cholesky | solution.py:64
  94.0 0.7 compare_reduce_fusion.4
  96.2 4.5 while.28
  96.5 0.6 fusion.108
  97.1 1.4 bitcast_dynamic-update-slice_fusion.6
  98.6 0.6 fusion.108
  99.2 1.4 bitcast_dynamic-update-slice_fusion.6
  100.7 19.7 %custom-call.17 = f32[2,128,128]{1,2,0:T(8,128)S(1)} custom-call(f32[2,128,128]{2,1,0:T(8,128)S(1)} %get-tuple-element.212), custom_call_target="InvertDiagBlocksLowerTriangular" | custom-call | tf_op jit(solution)/shard_map/triangular_solve/custom-call.0 | solution.py:32
  121.8 1.9 convolution_bitcast_fusion.3
  123.8 32.6 %all-reduce.10.cloned.1.call-done = f32[512,256]{0,1:T(8,128)} async-done(((f32[512,256]{0,1:T(8,128)}), f32[512,256]{0,1:T(8,128)}) %all-reduce.10.cloned.1.call-update) | async-done | bytes 524304 | tf_op jit(solution)/shard_map/psum | solution.py:41
  156.4 3.0 convolution_bitcast_fusion.2
  159.3 1.3 fusion.72
  161.1 43.7 %all-reduce.16.cloned.1.call-done = (f32[512,256]{0,1:T(8,128)}, f32[256,256]{0,1:T(8,128)}) async-done(((f32[512,256]{0,1:T(8,128)}, f32[256,256]{0,1:T(8,128)}), (f32[512,256]{0,1:T(8,128)}, f32[256,256]{0,1:T(8,128)})) %all-reduce.16.cloned.1.call-update) | async-done | bytes 786448 | tf_op jit(solution)/shard_map/psum | solution.py:63
  204.8 1.1 copy.47
  206.0 11.7 %cholesky.206 = f32[128,128]{1,0:T(8,128)S(1)} custom-call(f32[128,128]{1,0:T(8,128)S(1)} %cholesky.273), custom_call_target="Cholesky" | custom-call | tf_op jit(solution)/shard_map/jit(cholesky)/cholesky | solution.py:64
  217.8 9.8 %custom-call.18 = f32[1,128,128]{1,2,0:T(8,128)S(1)} custom-call(f32[1,128,128]{2,1,0:T(8,128)S(1)} %get-tuple-element.284), custom_call_target="InvertDiagBlocksLowerTriangular" | custom-call | tf_op jit(solution)/shard_map/jit(cholesky)/cholesky | solution.py:64
  228.1 11.7 %cholesky.223 = f32[128,128]{1,0:T(8,128)S(1)} custom-call(f32[128,128]{1,0:T(8,128)S(1)} %convolution_subtract_fusion.5), custom_call_target="Cholesky" | custom-call | tf_op jit(solution)/shard_map/jit(cholesky)/cholesky | solution.py:64
  239.8 0.7 compare_reduce_fusion.2
  240.5 0.7 compare_reduce_fusion.3
  242.6 16.1 %while.29 = (s32[]{:T(128)}, f32[256,256]{1,0:T(8,128)S(1)}, s32[2,2]{1,0:T(2,128)S(1)}, f32[2,128,128]{2,1,0:T(8,128)S(1)}, s32[]{:T(128)}) while((s32[]{:T(128)}, f32[256,256]{1,0:T(8,128)S(1)}, s32[2,2]{1,0:T(2,128)S(1)}, f32[2,128,128]{2,1,0:T(8,128)S(1)}, s32[]{:T(128)}) %tuple.129), condition=%wide.while_cond.clone, body=%wide.while_body.clone.sunk | while | flops 2 | bytes 131181 | solution.py:32
  254.5 0.6 fusion.109
  255.1 1.4 bitcast_dynamic-update-slice_fusion.7
  256.6 0.6 fusion.109
  257.3 1.4 bitcast_dynamic-update-slice_fusion.7
  258.7 19.7 %custom-call.19 = f32[2,128,128]{1,2,0:T(8,128)S(1)} custom-call(f32[2,128,128]{2,1,0:T(8,128)S(1)} %get-tuple-element.213), custom_call_target="InvertDiagBlocksLowerTriangular" | custom-call | tf_op jit(solution)/shard_map/triangular_solve/custom-call.0 | solution.py:32
  279.7 1.9 convolution_bitcast_fusion.1
  281.6 32.6 %all-reduce.12.cloned.1.call-done = f32[512,256]{0,1:T(8,128)} async-done(((f32[512,256]{0,1:T(8,128)}), f32[512,256]{0,1:T(8,128)}) %all-reduce.12.cloned.1.call-update) | async-done | bytes 524304 | tf_op jit(solution)/shard_map/psum | solution.py:41
  314.2 3.0 convolution_bitcast_fusion
  317.2 1.3 fusion.73
  318.6 0.9 copy-done.15
  319.4 0.7 copy.73
  320.2 0.6 copy-done.16
  321.1 1.6 reshape.164
  322.7 39.9 %all-reduce.14.cloned.1.call-done = (f32[512,256]{0,1:T(8,128)}, f32[256,256]{0,1:T(8,128)}) async-done(((f32[512,256]{0,1:T(8,128)}, f32[256,256]{0,1:T(8,128)}), (f32[512,256]{0,1:T(8,128)}, f32[256,256]{0,1:T(8,128)})) %all-reduce.14.cloned.1.call-update) | async-done | bytes 786448 | tf_op jit(solution)/shard_map/psum | solution.py:63
  362.6 1.1 copy.50
  363.8 11.7 %cholesky.240 = f32[128,128]{1,0:T(8,128)S(1)} custom-call(f32[128,128]{1,0:T(8,128)S(1)} %cholesky.276), custom_call_target="Cholesky" | custom-call | tf_op jit(solution)/shard_map/jit(cholesky)/cholesky | solution.py:64
  375.6 9.8 %custom-call.20 = f32[1,128,128]{1,2,0:T(8,128)S(1)} custom-call(f32[1,128,128]{2,1,0:T(8,128)S(1)} %get-tuple-element.280), custom_call_target="InvertDiagBlocksLowerTriangular" | custom-call | tf_op jit(solution)/shard_map/jit(cholesky)/cholesky | solution.py:64
  385.9 11.7 %cholesky.257 = f32[128,128]{1,0:T(8,128)S(1)} custom-call(f32[128,128]{1,0:T(8,128)S(1)} %convolution_subtract_fusion.4), custom_call_target="Cholesky" | custom-call | tf_op jit(solution)/shard_map/jit(cholesky)/cholesky | solution.py:64
  397.6 0.7 compare_reduce_fusion
  398.4 0.7 compare_reduce_fusion.1
  400.5 4.5 while.30
  401.3 1.4 bitcast_dynamic-update-slice_fusion.8
  402.8 0.6 fusion.110
  403.5 1.4 bitcast_dynamic-update-slice_fusion.8
  404.9 19.7 %custom-call.21 = f32[2,128,128]{1,2,0:T(8,128)S(1)} custom-call(f32[2,128,128]{2,1,0:T(8,128)S(1)} %get-tuple-element.214), custom_call_target="InvertDiagBlocksLowerTriangular" | custom-call | tf_op jit(solution)/shard_map/triangular_solve/custom-call.0 | solution.py:32
  426.6 1.1 fusion.61
  429.2 1.7 convolution_multiply_fusion
  430.9 1.9 select_reduce_fusion
  432.8 2.6 fusion.11
  436.0 13.2 %all_gather.10 = f32[4,1,32,16]{2,3,1,0:T(8,128)S(1)} all-gather(f32[1,1,32,16]{2,3,1,0:T(8,128)S(1)} %copy.57), channel_id=1, replica_groups=mesh['groups'=2,'tok'=4,'lay'=2,'head'=2] {'tok'}, dimensions={0}, use_global_device_ids=true | all-gather | bytes 10240 | tf_op jit(solution)/shard_map/all_gather | solution.py:15
  449.2 13.3 %all_gather.9 = f32[4,1,32,16]{2,3,1,0:T(8,128)S(1)} all-gather(f32[1,1,32,16]{2,3,1,0:T(8,128)S(1)} %copy.56), channel_id=1, replica_groups=mesh['groups'=2,'tok'=4,'lay'=2,'head'=2] {'tok'}, dimensions={0}, use_global_device_ids=true | all-gather | bytes 10240 | tf_op jit(solution)/shard_map/all_gather | solution.py:15
  462.5 1.0 all-gather.2.cloned.1.call-done
  463.5 1.0 slice_bitcast_fusion
  464.5 4.3 while.27
  464.7 1.2 fusion.107
  466.2 1.2 fusion.107
  467.6 1.2 fusion.107
  469.0 0.7 copy.61
  (122 shorter events, 11.1 us)
Async XLA Ops:
  6.5 3.0 copy-start
  6.5 3.0 copy-start.2
  6.5 52.4 %all-reduce.18.cloned.1.call-start = ((), (), s32[]{:S(2)}) async-start(), calls=%async_computation.5 | async-start | bytes 1572864 | tf_op jit(solution)/shard_map/psum | solution.py:63
  12.2 144.2 %all-reduce.10.cloned.1.call-start = ((), (), s32[]{:S(2)}) async-start(), calls=%async_computation | async-start | bytes 1048576 | tf_op jit(solution)/shard_map/psum | solution.py:41
  59.0 1.2 copy-start.6
  96.1 24.3 %copy-start.13 = (f32[512,256]{1,0:T(8,128)S(1)}, f32[512,256]{1,0:T(8,128)}, u32[]{:S(2)}) copy-start(f32[512,256]{1,0:T(8,128)} %get-tuple-element.265) | copy-start | bytes 1572868
  123.7 81.1 %all-reduce.16.cloned.1.call-start = ((), (), s32[]{:S(2)}) async-start(), calls=%async_computation.4 | async-start | bytes 1572864 | tf_op jit(solution)/shard_map/psum | solution.py:63
  156.4 3.0 copy-start.3
  160.7 153.5 %all-reduce.12.cloned.1.call-start = ((), (), s32[]{:S(2)}) async-start(), calls=%async_computation.1 | async-start | bytes 1048576 | tf_op jit(solution)/shard_map/psum | solution.py:41
  204.8 1.2 copy-start.7
  242.6 35.8 %copy-start.14 = (f32[512,256]{0,1:T(8,128)S(1)}, f32[512,256]{0,1:T(8,128)}, u32[]{:S(2)}) copy-start(f32[512,256]{0,1:T(8,128)} %get-tuple-element.263) | copy-start | bytes 1572868
  281.5 81.0 %all-reduce.14.cloned.1.call-start = ((), (), s32[]{:S(2)}) async-start(), calls=%async_computation.3 | async-start | bytes 1572864 | tf_op jit(solution)/shard_map/psum | solution.py:63
  314.2 3.0 copy-start.1
  318.5 0.9 copy-start.15
  318.5 145.0 %all-gather.2.cloned.1.call-start = ((), (), s32[]{:S(2)}) async-start(), calls=%async_computation.2 | async-start | bytes 1310720 | tf_op jit(solution)/shard_map/all_gather | solution.py:15
  320.2 0.7 copy-start.16
  362.6 1.2 copy-start.4
  363.8 11.7 %copy-start.8 = (f32[256,256]{1,0:T(8,128)}, f32[256,256]{1,0:T(8,128)S(1)}, u32[]{:S(2)}) copy-start(f32[256,256]{1,0:T(8,128)S(1)} %fusion.34) | copy-start | bytes 786436
  375.6 9.8 %copy-start.9 = (f32[256,256]{1,0:T(8,128)S(1)}, f32[256,256]{1,0:T(8,128)}, u32[]{:S(2)}) copy-start(f32[256,256]{1,0:T(8,128)} %copy-done.8) | copy-start | bytes 786436
  424.6 0.6 copy-start.10
  425.7 0.9 copy-start.11
  425.7 2.0 copy-start.12
  429.2 1.7 copy-start.5
Sparse Core Ops, SparseCore 0:
  12.3 46.5 all-reduce.17
  123.8 32.5 all-reduce.9
  160.8 43.8 all-reduce.15
  281.7 32.4 all-reduce.11
  318.6 43.8 all-reduce.13
  435.6 27.8 all-gather.1
where the time goes:
time: 480 us; the launch traced here: 477 us
  waiting for transfers between devices  196 us (41%)
  other arithmetic  167 us (35%)
  matrix products  31.4 us (7%)
  blocking collectives  26.5 us (6%)
  local copies, waits for them, and re-layouts  24 us (5%)
  between operations  18.3 us (4%)
  loops' own time  12.5 us (3%)
    psum x3, waiting for transfers between devices, finish(): gram, proj = lax.psum((gram_of(block), project(keys, block)), 'tok')  130 us
    another operation x20, other arithmetic, finish(): lower = jnp.linalg.cholesky(gram)  103 us
    psum x2, waiting for transfers between devices, mix_block(): return lax.psum(partial_block, ('lay', 'head'))  65.2 us
    another operation x8, other arithmetic, right_solve(): lax.linalg.triangular_solve(lower, matrix, left_side=False, lower=True, t...  59.2 us
    all_gather x2, blocking collectives, joined(): gathered = jax.tree.map(lambda a: lax.all_gather(a, axis), part)  26.5 us
    another operation x22, local copies, waits for them, and re-layouts, right_solve(): lax.linalg.triangular_solve(lower, matrix, left_side=False, lower=True, t...  12.7 us
    another operation x3, loops' own time, right_solve(): lax.linalg.triangular_solve(lower, matrix, left_side=False, lower=True, t...  12.4 us
  transfers between devices with their start and end apart: 6, of which 6 were waited for; matrix products, arithmetic and copies ran while one was open for 1% of the time, Pallas kernels for 0%

commit v1 on v0

--- a/solution.py
+++ b/solution.py
@@ -3,6 +3,7 @@
 import jax.numpy as jnp
 from jax import lax
 from jax.sharding import PartitionSpec as P
+from jax.lax import all_gather
 
 KVH = 8
 HD = 128
@@ -38,7 +39,7 @@
 
 def mix_block(keys, coef):
     partial_block = jnp.einsum("lsc,lcr->sr", keys, coef, precision=lax.Precision.HIGHEST)
-    return lax.psum(partial_block, ("lay", "head"))
+    return jnp.sum(all_gather(partial_block, axis_name=("lay", "head")), axis=0)
 
 
 def combine(first, second):

time: 480 us -> 464 us (0.967)
  waiting for transfers between devices: 196 us -> 176 us
  loops' own time: 12.5 us -> 0.93 us
  other arithmetic: 167 us -> 175 us
    psum x2 -> x0, waiting for transfers between devices: 65.2 us -> none  [mix_block(): return lax.psum(partial_block, ('lay', 'head'))]
    all_gather x0 -> x2, waiting for transfers between devices: none -> 44.1 us  [mix_block(): return jnp.sum(all_gather(partial_block, axis_name=('lay', 'head')), axis=0)]
    another operation x3, loops' own time: 12.4 us -> 0.79 us  [right_solve(): lax.linalg.triangular_solve(lower, matrix, left_side=False, lower=True, t...]
    all_gather x0 -> x2, local copies, waits for them, and re-layouts: none -> 6.31 us  [mix_block(): return jnp.sum(all_gather(partial_block, axis_name=('lay', 'head')), axis=0)]
    reduce_sum x0 -> x2, other arithmetic: none -> 4.96 us  [mix_block(): return jnp.sum(all_gather(partial_block, axis_name=('lay', 'head')), axis=0)]
    another operation x22 -> x23, local copies, waits for them, and re-layouts: 12.7 us -> 12.2 us  [right_solve(): lax.linalg.triangular_solve(lower, matrix, left_side=False, lower=True, t...]
where the time goes in v1:
time: 464 us; the launch traced here: 460 us
  waiting for transfers between devices  176 us (38%)
  other arithmetic  175 us (38%)
  matrix products  35.1 us (8%)
  local copies, waits for them, and re-layouts  28.7 us (6%)
  blocking collectives  26.5 us (6%)
  between operations  18 us (4%)
    psum x3, waiting for transfers between devices, finish(): gram, proj = lax.psum((gram_of(block), project(keys, block)), 'tok')  130 us
    another operation x20, other arithmetic, finish(): lower = jnp.linalg.cholesky(gram)  103 us
    another operation x8, other arithmetic, right_solve(): lax.linalg.triangular_solve(lower, matrix, left_side=False, lower=True, t...  59.2 us
    all_gather x2, waiting for transfers between devices, mix_block(): return jnp.sum(all_gather(partial_block, axis_name=('lay', 'head')), axis=0)  44.1 us
    all_gather x2, blocking collectives, joined(): gathered = jax.tree.map(lambda a: lax.all_gather(a, axis), part)  26.5 us
    another operation x23, local copies, waits for them, and re-layouts, right_solve(): lax.linalg.triangular_solve(lower, matrix, left_side=False, lower=True, t...  12.2 us
  transfers between devices with their start and end apart: 6, of which 6 were waited for; matrix products, arithmetic and copies ran while one was open for 1% of the time, Pallas kernels for 0%

profile of v1, /device:TPU:0, one launch (start us, length us, event | category | flops | bytes accessed | tf_op | source)
XLA Modules:
  0.0 460.3 jit_solution(3311239385310967649)
XLA Ops:
  6.5 3.0 fusion.71
  9.5 3.7 fusion.9
  13.5 46.5 %all-reduce.12.cloned.1.call-done = (f32[512,256]{1,0:T(8,128)}, f32[256,256]{0,1:T(8,128)}) async-done(((f32[512,256]{1,0:T(8,128)}, f32[256,256]{0,1:T(8,128)}), (f32[512,256]{1,0:T(8,128)}, f32[256,256]{0,1:T(8,128)})) %all-reduce.12.cloned.1.call-update) | async-done | bytes 786448 | tf_op jit(solution)/shard_map/psum | solution.py:64
  60.0 1.1 copy.45
  61.1 1.0 fusion.36
  62.1 11.7 %cholesky.172 = f32[128,128]{1,0:T(8,128)S(1)} custom-call(f32[128,128]{1,0:T(8,128)S(1)} %cholesky.270), custom_call_target="Cholesky" | custom-call | tf_op jit(solution)/shard_map/jit(cholesky)/cholesky | solution.py:65
  73.9 9.8 %custom-call.16 = f32[1,128,128]{1,2,0:T(8,128)S(1)} custom-call(f32[1,128,128]{2,1,0:T(8,128)S(1)} %get-tuple-element.288), custom_call_target="InvertDiagBlocksLowerTriangular" | custom-call | tf_op jit(solution)/shard_map/jit(cholesky)/cholesky | solution.py:65
  84.2 11.7 %cholesky.189 = f32[128,128]{1,0:T(8,128)S(1)} custom-call(f32[128,128]{1,0:T(8,128)S(1)} %convolution_subtract_fusion.6), custom_call_target="Cholesky" | custom-call | tf_op jit(solution)/shard_map/jit(cholesky)/cholesky | solution.py:65
  96.0 0.7 compare_reduce_fusion.4
  98.1 4.3 while.28
  99.0 1.3 bitcast_dynamic-update-slice_fusion.6
  101.0 1.3 bitcast_dynamic-update-slice_fusion.6
  102.4 19.7 %custom-call.17 = f32[2,128,128]{1,2,0:T(8,128)S(1)} custom-call(f32[2,128,128]{2,1,0:T(8,128)S(1)} %get-tuple-element.212), custom_call_target="InvertDiagBlocksLowerTriangular" | custom-call | tf_op jit(solution)/shard_map/triangular_solve/custom-call.0 | solution.py:33
  123.5 1.9 convolution_bitcast_fusion.3
  125.4 22.0 %all-gather.8.cloned.1.call-done = f32[2048,256]{0,1:T(8,128)} async-done(((f32[512,256]{0,1:T(8,128)}), f32[2048,256]{0,1:T(8,128)}) %all-gather.8.cloned.1.call-update) | async-done | bytes 2097168 | tf_op jit(solution)/shard_map/all_gather | solution.py:42
  147.5 2.7 reshape.203
  150.1 2.1 reduce_sum.27
  152.3 3.0 convolution_bitcast_fusion.2
  155.3 1.3 fusion.72
  157.1 43.6 %all-reduce.10.cloned.1.call-done = (f32[512,256]{0,1:T(8,128)}, f32[256,256]{0,1:T(8,128)}) async-done(((f32[512,256]{0,1:T(8,128)}, f32[256,256]{0,1:T(8,128)}), (f32[512,256]{0,1:T(8,128)}, f32[256,256]{0,1:T(8,128)})) %all-reduce.10.cloned.1.call-update) | async-done | bytes 786448 | tf_op jit(solution)/shard_map/psum | solution.py:64
  200.7 1.1 copy.47
  201.8 1.0 fusion.35
  202.8 11.7 %cholesky.206 = f32[128,128]{1,0:T(8,128)S(1)} custom-call(f32[128,128]{1,0:T(8,128)S(1)} %cholesky.273), custom_call_target="Cholesky" | custom-call | tf_op jit(solution)/shard_map/jit(cholesky)/cholesky | solution.py:65
  214.6 9.8 %custom-call.18 = f32[1,128,128]{1,2,0:T(8,128)S(1)} custom-call(f32[1,128,128]{2,1,0:T(8,128)S(1)} %get-tuple-element.284), custom_call_target="InvertDiagBlocksLowerTriangular" | custom-call | tf_op jit(solution)/shard_map/jit(cholesky)/cholesky | solution.py:65
  224.9 11.7 %cholesky.223 = f32[128,128]{1,0:T(8,128)S(1)} custom-call(f32[128,128]{1,0:T(8,128)S(1)} %convolution_subtract_fusion.5), custom_call_target="Cholesky" | custom-call | tf_op jit(solution)/shard_map/jit(cholesky)/cholesky | solution.py:65
  237.3 0.7 compare_reduce_fusion.3
  239.3 4.3 while.29
  240.2 1.3 bitcast_dynamic-update-slice_fusion.7
  242.2 1.3 bitcast_dynamic-update-slice_fusion.7
  243.6 19.7 %custom-call.19 = f32[2,128,128]{1,2,0:T(8,128)S(1)} custom-call(f32[2,128,128]{2,1,0:T(8,128)S(1)} %get-tuple-element.213), custom_call_target="InvertDiagBlocksLowerTriangular" | custom-call | tf_op jit(solution)/shard_map/triangular_solve/custom-call.0 | solution.py:33
  264.5 1.9 convolution_bitcast_fusion.1
  266.4 22.0 %all-gather.10.cloned.1.call-done = f32[2048,256]{0,1:T(8,128)} async-done(((f32[512,256]{0,1:T(8,128)}), f32[2048,256]{0,1:T(8,128)}) %all-gather.10.cloned.1.call-update) | async-done | bytes 2097168 | tf_op jit(solution)/shard_map/all_gather | solution.py:42
  288.5 3.6 reshape.204
  292.1 2.8 reduce_sum.28
  295.0 1.9 convolution_bitcast_fusion
  296.8 1.3 fusion.73
  298.5 0.8 copy.73
  299.5 1.6 reshape.164
  301.1 0.9 copy.72
  302.0 40.3 %all-reduce.8.cloned.1.call-done = (f32[512,256]{0,1:T(8,128)}, f32[256,256]{0,1:T(8,128)}) async-done(((f32[512,256]{0,1:T(8,128)}, f32[256,256]{0,1:T(8,128)}), (f32[512,256]{0,1:T(8,128)}, f32[256,256]{0,1:T(8,128)})) %all-reduce.8.cloned.1.call-update) | async-done | bytes 786448 | tf_op jit(solution)/shard_map/psum | solution.py:64
  342.2 1.1 copy.50
  343.3 1.0 fusion.34
  344.3 11.7 %cholesky.240 = f32[128,128]{1,0:T(8,128)S(1)} custom-call(f32[128,128]{1,0:T(8,128)S(1)} %cholesky.276), custom_call_target="Cholesky" | custom-call | tf_op jit(solution)/shard_map/jit(cholesky)/cholesky | solution.py:65
  356.1 9.8 %custom-call.20 = f32[1,128,128]{1,2,0:T(8,128)S(1)} custom-call(f32[1,128,128]{2,1,0:T(8,128)S(1)} %get-tuple-element.280), custom_call_target="InvertDiagBlocksLowerTriangular" | custom-call | tf_op jit(solution)/shard_map/jit(cholesky)/cholesky | solution.py:65
  366.4 11.7 %cholesky.257 = f32[128,128]{1,0:T(8,128)S(1)} custom-call(f32[128,128]{1,0:T(8,128)S(1)} %convolution_subtract_fusion.4), custom_call_target="Cholesky" | custom-call | tf_op jit(solution)/shard_map/jit(cholesky)/cholesky | solution.py:65
  378.8 0.7 compare_reduce_fusion.1
  380.8 4.3 while.30
  381.8 1.3 bitcast_dynamic-update-slice_fusion.8
  383.8 1.3 bitcast_dynamic-update-slice_fusion.8
  385.2 19.7 %custom-call.21 = f32[2,128,128]{1,2,0:T(8,128)S(1)} custom-call(f32[2,128,128]{2,1,0:T(8,128)S(1)} %get-tuple-element.214), custom_call_target="InvertDiagBlocksLowerTriangular" | custom-call | tf_op jit(solution)/shard_map/triangular_solve/custom-call.0 | solution.py:33
  405.9 1.6 convolution_subtract_fusion.1
  407.5 2.0 fusion.61
  409.5 1.3 fusion.26
  411.8 1.7 convolution_multiply_fusion
  413.5 2.8 select_reduce_fusion
  416.3 2.7 fusion.11
  419.5 13.2 %all_gather.26 = f32[4,1,32,16]{2,3,1,0:T(8,128)S(1)} all-gather(f32[1,1,32,16]{2,3,1,0:T(8,128)S(1)} %copy.57), channel_id=1, replica_groups=mesh['groups'=2,'tok'=4,'lay'=2,'head'=2] {'tok'}, dimensions={0}, use_global_device_ids=true | all-gather | bytes 10240 | tf_op jit(solution)/shard_map/all_gather | solution.py:16
  432.7 13.3 %all_gather.25 = f32[4,1,32,16]{2,3,1,0:T(8,128)S(1)} all-gather(f32[1,1,32,16]{2,3,1,0:T(8,128)S(1)} %copy.56), channel_id=1, replica_groups=mesh['groups'=2,'tok'=4,'lay'=2,'head'=2] {'tok'}, dimensions={0}, use_global_device_ids=true | all-gather | bytes 10240 | tf_op jit(solution)/shard_map/all_gather | solution.py:16
  446.0 1.0 all-gather.6.cloned.1.call-done
  447.1 1.0 slice_bitcast_fusion
  448.0 4.3 while.27
  448.3 1.2 fusion.107
  449.7 1.2 fusion.107
  451.2 1.2 fusion.107
  (112 shorter events, 15.2 us)
Async XLA Ops:
  6.5 3.0 copy-start
  6.5 53.4 %all-reduce.12.cloned.1.call-start = ((), (), s32[]{:S(2)}) async-start(), calls=%async_computation.5 | async-start | bytes 1572864 | tf_op jit(solution)/shard_map/psum | solution.py:64
  13.2 134.2 %all-gather.8.cloned.1.call-start = ((), (), s32[]{:S(2)}) async-start(), calls=%async_computation.1 | async-start | bytes 2621440 | tf_op jit(solution)/shard_map/all_gather | solution.py:42
  60.0 62.1 %copy-start.5 = (f32[512,256]{1,0:T(8,128)S(1)}, f32[512,256]{1,0:T(8,128)}, u32[]{:S(2)}) copy-start(f32[512,256]{1,0:T(8,128)} %get-tuple-element.265) | copy-start | bytes 1572868
  125.4 75.3 %all-reduce.10.cloned.1.call-start = ((), (), s32[]{:S(2)}) async-start(), calls=%async_computation.4 | async-start | bytes 1572864 | tf_op jit(solution)/shard_map/psum | solution.py:64
  152.3 3.0 copy-start.1
  156.6 131.9 %all-gather.10.cloned.1.call-start = ((), (), s32[]{:S(2)}) async-start(), calls=%async_computation.2 | async-start | bytes 2621440 | tf_op jit(solution)/shard_map/all_gather | solution.py:42
  200.7 62.6 %copy-start.6 = (f32[512,256]{0,1:T(8,128)S(1)}, f32[512,256]{0,1:T(8,128)}, u32[]{:S(2)}) copy-start(f32[512,256]{0,1:T(8,128)} %get-tuple-element.263) | copy-start | bytes 1572868
  266.4 75.8 %all-reduce.8.cloned.1.call-start = ((), (), s32[]{:S(2)}) async-start(), calls=%async_computation.3 | async-start | bytes 1572864 | tf_op jit(solution)/shard_map/psum | solution.py:64
  295.0 3.5 copy-start.7
  295.0 4.3 copy-start.8
  298.2 148.9 %all-gather.6.cloned.1.call-start = ((), (), s32[]{:S(2)}) async-start(), calls=%async_computation | async-start | bytes 1310720 | tf_op jit(solution)/shard_map/all_gather | solution.py:16
  404.9 0.7 copy-start.2
  405.5 4.0 copy-start.4
  405.9 5.2 %copy-start.3 = (f32[2,128,128]{1,2,0:T(8,128)S(1)}, f32[2,128,128]{1,2,0:T(8,128)}, u32[]{:S(2)}) copy-start(f32[2,128,128]{1,2,0:T(8,128)} %copy-done.2) | copy-start | bytes 393220
Sparse Core Ops, SparseCore 0:
  13.4 46.5 all-reduce.11
  125.5 21.9 all-gather.7
  156.7 43.8 all-reduce.9
  266.5 21.9 all-gather.9
  298.3 43.8 all-reduce.7
  419.2 27.8 all-gather.5
